TPU v7x, 32 devices: a whole 2x2x4 slice. The times are simulated.
32 devices in a mesh: src: 4 (over x, core), dst: 2 (over y), tm: 4 (over z).
Axes of the slice: x: 2, y: 2, z: 4, core: 2. Of those that a mesh axis runs over, the one named last changes fastest.
Arguments:
- traffic: bfloat16 [256, 256, 512], P('src', 'dst', 'tm'), may hold values from -6 to 6
- src_factor: float32 [256, 64], P('src'), may hold values from -0.75 to 0.75
- dst_factor: float32 [256, 64], P('dst'), may hold values from -0.75 to 0.75
- time_factor: float32 [512, 64], P('tm'), may hold values from -0.75 to 0.75
Outputs:
- grad_src: float32 [256, 64], P('src')
- grad_dst: float32 [256, 64], P('dst')
- grad_time: float32 [512, 64], P('tm')
All inputs are finite; a program needn't handle non-finite values.
Results may differ from a plain program's by a relative error of at most 0.0003.
Values sent between devices are 32-bit elements; how exact they have to be, the bound alone decides.
No kernel may reach another device: no remote copies, remote signals or barrier semaphores. Data moves between devices by JAX's collectives and lax.ppermute only.
A program may use at most 64 MiB of HBM per device.

v0:
```python
import jax
import jax.numpy as jnp
from jax import lax
from jax.sharding import PartitionSpec as P

DAY = 288
STEPS = 3
hour_weight = 32.0
day_weight = 64.0
step_rate = 0.1
highest = lax.Precision.HIGHEST


def passed_along(block, axis, distance):
    devices = range(lax.axis_size(axis))
    route = [(i - distance, i) for i in devices if i - distance in devices]
    return lax.ppermute(block, axis, route)


def behind(values, offset):
    row_count = values.shape[0]
    whole_blocks, extra_rows = divmod(offset, row_count)
    pieces = []
    for part_by, first_row, last_row in (
        (whole_blocks + 1, row_count - extra_rows, row_count),
        (whole_blocks, 0, row_count - extra_rows),
    ):
        block_rows = values[first_row:last_row]
        if part_by == 0:
            pieces.append(block_rows)
        else:
            pieces.append(passed_along(block_rows, "tm", part_by))
    return jnp.concatenate(pieces, 0)


def ahead(values, offset):
    row_count = values.shape[0]
    whole_blocks, extra_rows = divmod(offset, row_count)
    pieces = []
    for part_by, first_row, last_row in (
        (-whole_blocks, extra_rows, row_count),
        (-(whole_blocks + 1), 0, extra_rows),
    ):
        block_rows = values[first_row:last_row]
        if part_by == 0:
            pieces.append(block_rows)
        else:
            pieces.append(passed_along(block_rows, "tm", part_by))
    return jnp.concatenate(pieces, 0)


def smoothing(time_now, position):
    hour_diff = jnp.where((position >= 1)[:, None], time_now - behind(time_now, 1), 0.0)
    day_diff = jnp.where((position >= DAY)[:, None], time_now - behind(time_now, DAY), 0.0)
    hour_next = ahead(hour_diff, 1)
    day_next = ahead(day_diff, DAY)
    return hour_weight * (hour_diff - hour_next) + day_weight * (day_diff - day_next)


def on_device(traffic, src_factor, dst_factor, time_factor):
    src_rows, rank_count = src_factor.shape
    dst_rows = dst_factor.shape[0]
    time_rows = time_factor.shape[0]
    position = lax.axis_index("tm") * time_rows + jnp.arange(time_rows, dtype=jnp.int32)
    observed = traffic.reshape(src_rows, dst_rows * time_rows)
    src_now, dst_now, time_now = (src_factor, dst_factor, time_factor)
    for iteration in range(STEPS):
        dst_time = (dst_now.T[:, :, None] * time_now.T[:, None, :]).reshape(
            rank_count, dst_rows * time_rows
        )
        model_cells = jnp.dot(src_now, dst_time, precision=highest)
        residual = model_cells - observed.astype(jnp.float32)
        raw_src = jnp.einsum("ix,rx->ir", residual, dst_time, precision=highest)
        resid_cube = residual.reshape(src_rows, dst_rows, time_rows)
        src_time = src_now.T[:, :, None] * time_now.T[:, None, :]
        raw_dst = jnp.einsum("ijk,rik->jr", resid_cube, src_time, precision=highest)
        src_dst = src_now.T[:, :, None] * dst_now.T[:, None, :]
        raw_time = jnp.einsum("ijk,rij->kr", resid_cube, src_dst, precision=highest)
        grad_src = lax.psum(raw_src, ("dst", "tm")) / rank_count
        grad_dst = lax.psum(raw_dst, ("src", "tm")) / rank_count
        summed_time = lax.psum(raw_time, ("src", "dst"))
        grad_time = (summed_time + smoothing(time_now, position)) / rank_count
        if iteration + 1 < STEPS:
            src_now = src_now - step_rate * grad_src
            dst_now = dst_now - step_rate * grad_dst
            time_now = time_now - step_rate * grad_time
    return (grad_src, grad_dst, grad_time)


def solution(mesh):
    in_specs = (P("src", "dst", "tm"), P("src", None), P("dst", None), P("tm", None))
    out_specs = (P("src", None), P("dst", None), P("tm", None))
    return jax.shard_map(
        on_device, mesh=mesh, in_specs=in_specs, out_specs=out_specs, check_vma=False
    )
```

profile of v0, /device:TPU:27, one launch (start us, length us, event | category | flops | bytes accessed | tf_op | source)
XLA Modules:
  0.0 477.5 jit_solution(11695391213092118398)
XLA Ops:
  0.7 0.9 slice.72
  1.5 1.3 collective-permute-start
  2.8 0.8 slice.76
  3.7 1.3 collective-permute-start.2
  5.0 1.3 collective-permute-start.3
  6.3 2.1 convert.1
  8.4 1.2 broadcast_multiply_fusion.2
  9.6 8.5 %fusion = f32[64,16384]{1,0:T(8,128)S(1)} fusion(f32[64,64]{1,0:T(8,128)S(1)} %copy-done.4, f32[8,8,128,128]{3,2,1,0:T(8,128)S(1)} %bitcast.86, f32[8,8,128,128]{3,2,1,0:T(8,128)S(1)} %convert.1), kind=kOutput, calls=%fused_computation.3 | convolution fusion | flops 806354944 | bytes 12599296 | tf_op jit(solution)/shard_map/dot_general | solution.py:71
  18.1 14.4 %fusion.7 = f32[64,64]{1,0:T(8,128)S(1)} fusion(f32[64,16384]{1,0:T(8,128)S(1)} %fusion, f32[8,8,128,128]{3,2,1,0:T(8,128)S(1)} %bitcast.87), kind=kOutput, calls=%fused_computation.10 | convolution fusion | flops 805306368 | bytes 8404992 | tf_op jit(solution)/shard_map/ix,rx->ir/dot_general | solution.py:73
  32.6 0.7 copy.9
  33.3 2.9 fusion.31
  36.3 4.5 fusion.28
  40.7 26.9 %psum.63 = f32[64,64]{1,0:T(8,128)S(1)} all-reduce(f32[64,64]{1,0:T(8,128)S(1)} %fusion.7), channel_id=1, replica_groups=mesh['src'=4,'dst'=2,'tm'=4] {'dst','tm'}, use_global_device_ids=true, to_apply=%region_0.0 | all-reduce | flops 4096 | bytes 32768 | tf_op jit(solution)/shard_map/psum | solution.py:79
  67.7 64.5 %psum.64 = f32[128,64]{0,1:T(8,128)S(1)} all-reduce(f32[128,64]{0,1:T(8,128)S(1)} %fusion.28), channel_id=1, replica_groups=mesh['src'=4,'dst'=2,'tm'=4] {'src','tm'}, use_global_device_ids=true, to_apply=%region_1.0 | all-reduce | flops 8192 | bytes 65536 | tf_op jit(solution)/shard_map/psum | solution.py:80
  132.4 1.7 collective-permute-start.4
  134.1 4.0 collective-permute-start.1
  138.1 1.3 collective-permute-start.5
  139.4 27.7 %psum.65 = f32[128,64]{0,1:T(8,128)S(1)} all-reduce(f32[128,64]{0,1:T(8,128)S(1)} %fusion.31), channel_id=1, replica_groups=mesh['src'=4,'dst'=2,'tm'=4] {'src','dst'}, use_global_device_ids=true, to_apply=%region_2.0 | all-reduce | flops 8192 | bytes 65536 | tf_op jit(solution)/shard_map/psum | solution.py:81
  167.5 1.2 broadcast_multiply_fusion.1
  169.3 8.1 %convolution_subtract_fusion.1 = f32[64,16384]{1,0:T(8,128)S(1)} fusion(f32[64,64]{1,0:T(8,128)S(1)} %multiply_subtract_fusion.2, f32[8,8,128,128]{3,2,1,0:T(8,128)S(1)} %bitcast.88, f32[8,8,128,128]{3,2,1,0:T(8,128)S(1)} %copy-done.1), kind=kOutput, calls=%fused_computation.1 | convolution fusion | flops 806354944 | bytes 12599296 | tf_op jit(solution)/shard_map/dot_general | solution.py:71
  177.4 6.0 %fusion.4 = f32[64,64]{1,0:T(8,128)S(1)} fusion(f32[64,16384]{1,0:T(8,128)S(1)} %convolution_subtract_fusion.1, f32[8,8,128,128]{3,2,1,0:T(8,128)S(1)} %bitcast.89), kind=kOutput, calls=%fused_computation.7 | convolution fusion | flops 805306368 | bytes 8404992 | tf_op jit(solution)/shard_map/ix,rx->ir/dot_general | solution.py:73
  183.5 0.7 copy.11
  184.2 2.9 fusion.37
  187.2 4.5 fusion.34
  191.6 1.3 collective-permute-start.6
  192.9 1.3 collective-permute-start.8
  194.2 1.3 collective-permute-start.9
  195.5 58.0 %psum.67 = f32[128,64]{0,1:T(8,128)S(1)} all-reduce(f32[128,64]{0,1:T(8,128)S(1)} %fusion.34), channel_id=1, replica_groups=mesh['src'=4,'dst'=2,'tm'=4] {'src','tm'}, use_global_device_ids=true, to_apply=%region_4.5 | all-reduce | flops 8192 | bytes 65536 | tf_op jit(solution)/shard_map/psum | solution.py:80
  253.5 25.8 %psum.66 = f32[64,64]{1,0:T(8,128)S(1)} all-reduce(f32[64,64]{1,0:T(8,128)S(1)} %fusion.4), channel_id=1, replica_groups=mesh['src'=4,'dst'=2,'tm'=4] {'dst','tm'}, use_global_device_ids=true, to_apply=%region_3.4 | all-reduce | flops 4096 | bytes 32768 | tf_op jit(solution)/shard_map/psum | solution.py:79
  279.5 1.5 collective-permute-start.10
  281.0 6.3 %collective-permute-start.7 = (f32[1,64]{0,1:T(8,128)S(1)}, f32[1,64]{0,1:T(8,128)S(1)}, u32[]{:S(2)}, u32[]{:S(2)}) collective-permute-start(f32[1,64]{0,1:T(8,128)S(1)} %bitcast.116), channel_id=1, source_target_pairs={{1,0},{2,1},{3,2},{5,4},{6,5},{7,6},{9,8},{10,9},{11,10},{13,12},{... | collective-permute-start | bytes 776 | tf_op jit(solution)/shard_map/ppermute | solution.py:17
  287.3 1.3 collective-permute-start.11
  288.6 32.4 %psum.68 = f32[128,64]{0,1:T(8,128)S(1)} all-reduce(f32[128,64]{0,1:T(8,128)S(1)} %fusion.37), channel_id=1, replica_groups=mesh['src'=4,'dst'=2,'tm'=4] {'src','dst'}, use_global_device_ids=true, to_apply=%region_5.6 | all-reduce | flops 8192 | bytes 65536 | tf_op jit(solution)/shard_map/psum | solution.py:81
  321.4 1.2 broadcast_multiply_fusion
  323.2 8.1 %convolution_subtract_fusion = f32[64,16384]{1,0:T(8,128)S(1)} fusion(f32[8,8,128,128]{3,2,1,0:T(8,128)S(1)} %bitcast.82, f32[8,8,128,128]{3,2,1,0:T(8,128)S(1)} %copy-done.2, f32[64,64]{1,0:T(8,128)S(1)} %multiply_subtract_fusion.2, f32[64,64]{1,0:T(8,128)S(1)} %psum.66), kind=kOutput, calls=%fused_computation | convolution fusion | flops 806363136 | bytes 12615680 | tf_op jit(solution)/shard_map/dot_general | solution.py:71
  331.3 5.8 %fusion.1 = f32[64,64]{1,0:T(8,128)S(1)} fusion(f32[64,16384]{1,0:T(8,128)S(1)} %convolution_subtract_fusion, f32[8,8,128,128]{3,2,1,0:T(8,128)S(1)} %bitcast.83), kind=kOutput, calls=%fused_computation.4 | convolution fusion | flops 805306368 | bytes 8404992 | tf_op jit(solution)/shard_map/ix,rx->ir/dot_general | solution.py:73
  337.2 0.7 copy.13
  338.0 2.9 fusion.43
  340.9 4.5 fusion.40
  345.4 1.3 collective-permute-start.12
  346.7 1.3 collective-permute-start.14
  348.0 1.3 collective-permute-start.15
  349.3 26.0 %psum.69 = f32[64,64]{1,0:T(8,128)S(1)} all-reduce(f32[64,64]{1,0:T(8,128)S(1)} %fusion.1), channel_id=1, replica_groups=mesh['src'=4,'dst'=2,'tm'=4] {'dst','tm'}, use_global_device_ids=true, to_apply=%region_6.7 | all-reduce | flops 4096 | bytes 32768 | tf_op jit(solution)/shard_map/psum | solution.py:79
  375.9 65.0 %psum.70 = f32[128,64]{0,1:T(8,128)S(1)} all-reduce(f32[128,64]{0,1:T(8,128)S(1)} %fusion.40), channel_id=1, replica_groups=mesh['src'=4,'dst'=2,'tm'=4] {'src','tm'}, use_global_device_ids=true, to_apply=%region_7.8 | all-reduce | flops 8192 | bytes 65536 | tf_op jit(solution)/shard_map/psum | solution.py:80
  441.1 1.8 collective-permute-start.16
  443.6 4.0 collective-permute-start.13
  447.5 1.3 collective-permute-start.17
  448.8 27.5 %psum.71 = f32[128,64]{0,1:T(8,128)S(1)} all-reduce(f32[128,64]{0,1:T(8,128)S(1)} %fusion.43), channel_id=1, replica_groups=mesh['src'=4,'dst'=2,'tm'=4] {'src','dst'}, use_global_device_ids=true, to_apply=%region_8.9 | all-reduce | flops 8192 | bytes 65536 | tf_op jit(solution)/shard_map/psum | solution.py:81
  (53 shorter events, 4.6 us)
Async XLA Ops:
  0.6 7.8 %copy-start.3 = (f32[128,64]{0,1:T(8,128)S(1)}, f32[128,64]{0,1:T(8,128)}, u32[]{:S(2)}) copy-start(f32[128,64]{0,1:T(8,128)} %param.7) | copy-start | bytes 98308
  0.6 7.8 %copy-start.5 = (f32[128,64]{0,1:T(8,128)S(1)}, f32[128,64]{0,1:T(8,128)}, u32[]{:S(2)}) copy-start(f32[128,64]{0,1:T(8,128)} %param.6) | copy-start | bytes 98308
  1.5 130.6 %collective-permute-start = (f32[1,64]{0,1:T(8,128)S(1)}, f32[1,64]{0,1:T(8,128)S(1)}, u32[]{:S(2)}, u32[]{:S(2)}) collective-permute-start(f32[1,64]{0,1:T(8,128)S(1)} %slice.72), channel_id=1, source_target_pairs={{0,1},{1,2},{2,3},{4,5},{5,6},{6,7},{8,9},{9,10},{10,11},{12,13},{... | collective-permute-start | bytes 776 | tf_op jit(solution)/shard_map/ppermute | solution.py:17
  3.7 128.5 %collective-permute-start.2 = (f32[32,64]{0,1:T(8,128)S(1)}, f32[32,64]{0,1:T(8,128)S(1)}, u32[]{:S(2)}, u32[]{:S(2)}) collective-permute-start(f32[32,64]{0,1:T(8,128)S(1)} %slice.76), channel_id=1, source_target_pairs={{0,3},{4,7},{8,11},{12,15},{16,19},{20,23},{24,27},{28,31}} | collective-permute-start | bytes 24584 | tf_op jit(solution)/shard_map/ppermute | solution.py:17
  5.0 127.2 %collective-permute-start.3 = (f32[96,64]{0,1:T(8,128)}, f32[96,64]{0,1:T(8,128)S(1)}, u32[]{:S(2)}, u32[]{:S(2)}) collective-permute-start(f32[96,64]{0,1:T(8,128)} %bitcast.101), channel_id=1, source_target_pairs={{0,2},{1,3},{4,6},{5,7},{8,10},{9,11},{12,14},{13,15},{16,18},{17,... | collective-permute-start | bytes 73736 | tf_op jit(solution)/shard_map/ppermute | solution.py:17
  6.3 3.3 copy-start.4
  8.4 9.7 %copy-start = (f32[8,8,128,128]{3,2,1,0:T(8,128)}, f32[8,8,128,128]{3,2,1,0:T(8,128)S(1)}, u32[]{:S(2)}) copy-start(f32[8,8,128,128]{3,2,1,0:T(8,128)S(1)} %convert.1) | copy-start | bytes 12582916
  132.4 34.9 %collective-permute-start.4 = (f32[96,64]{0,1:T(8,128)S(1)}, f32[96,64]{0,1:T(8,128)S(1)}, u32[]{:S(2)}, u32[]{:S(2)}) collective-permute-start(f32[96,64]{0,1:T(8,128)S(1)} %slice.98), channel_id=1, source_target_pairs={{2,0},{3,1},{6,4},{7,5},{10,8},{11,9},{14,12},{15,13},{18,16},{19,... | collective-permute-start | bytes 73736 | tf_op jit(solution)/shard_map/ppermute | solution.py:17
  134.1 33.1 %collective-permute-start.1 = (f32[1,64]{0,1:T(8,128)S(1)}, f32[1,64]{0,1:T(8,128)S(1)}, u32[]{:S(2)}, u32[]{:S(2)}) collective-permute-start(f32[1,64]{0,1:T(8,128)S(1)} %bitcast.118), channel_id=1, source_target_pairs={{1,0},{2,1},{3,2},{5,4},{6,5},{7,6},{9,8},{10,9},{11,10},{13,12},{... | collective-permute-start | bytes 776 | tf_op jit(solution)/shard_map/ppermute | solution.py:17
  138.1 29.1 %collective-permute-start.5 = (f32[32,64]{0,1:T(8,128)S(1)}, f32[32,64]{0,1:T(8,128)S(1)}, u32[]{:S(2)}, u32[]{:S(2)}) collective-permute-start(f32[32,64]{0,1:T(8,128)S(1)} %bitcast.117), channel_id=1, source_target_pairs={{3,0},{7,4},{11,8},{15,12},{19,16},{23,20},{27,24},{31,28}} | collective-permute-start | bytes 24584 | tf_op jit(solution)/shard_map/ppermute | solution.py:17
  167.1 2.2 copy-start.1
  191.6 87.7 %collective-permute-start.6 = (f32[1,64]{0,1:T(8,128)S(1)}, f32[1,64]{0,1:T(8,128)S(1)}, u32[]{:S(2)}, u32[]{:S(2)}) collective-permute-start(f32[1,64]{0,1:T(8,128)S(1)} %slice.100), channel_id=1, source_target_pairs={{0,1},{1,2},{2,3},{4,5},{5,6},{6,7},{8,9},{9,10},{10,11},{12,13},{... | collective-permute-start | bytes 776 | tf_op jit(solution)/shard_map/ppermute | solution.py:17
  192.9 86.4 %collective-permute-start.8 = (f32[32,64]{0,1:T(8,128)S(1)}, f32[32,64]{0,1:T(8,128)S(1)}, u32[]{:S(2)}, u32[]{:S(2)}) collective-permute-start(f32[32,64]{0,1:T(8,128)S(1)} %slice.104), channel_id=1, source_target_pairs={{0,3},{4,7},{8,11},{12,15},{16,19},{20,23},{24,27},{28,31}} | collective-permute-start | bytes 24584 | tf_op jit(solution)/shard_map/ppermute | solution.py:17
  194.2 85.1 %collective-permute-start.9 = (f32[96,64]{0,1:T(8,128)S(1)}, f32[96,64]{0,1:T(8,128)S(1)}, u32[]{:S(2)}, u32[]{:S(2)}) collective-permute-start(f32[96,64]{0,1:T(8,128)S(1)} %bitcast.98), channel_id=1, source_target_pairs={{0,2},{1,3},{4,6},{5,7},{8,10},{9,11},{12,14},{13,15},{16,18},{17,... | collective-permute-start | bytes 73736 | tf_op jit(solution)/shard_map/ppermute | solution.py:17
  279.5 41.6 %collective-permute-start.10 = (f32[96,64]{0,1:T(8,128)S(1)}, f32[96,64]{0,1:T(8,128)S(1)}, u32[]{:S(2)}, u32[]{:S(2)}) collective-permute-start(f32[96,64]{0,1:T(8,128)S(1)} %slice.106), channel_id=1, source_target_pairs={{2,0},{3,1},{6,4},{7,5},{10,8},{11,9},{14,12},{15,13},{18,16},{19,... | collective-permute-start | bytes 73736 | tf_op jit(solution)/shard_map/ppermute | solution.py:17
  281.0 40.1 %collective-permute-start.7 = (f32[1,64]{0,1:T(8,128)S(1)}, f32[1,64]{0,1:T(8,128)S(1)}, u32[]{:S(2)}, u32[]{:S(2)}) collective-permute-start(f32[1,64]{0,1:T(8,128)S(1)} %bitcast.116), channel_id=1, source_target_pairs={{1,0},{2,1},{3,2},{5,4},{6,5},{7,6},{9,8},{10,9},{11,10},{13,12},{... | collective-permute-start | bytes 776 | tf_op jit(solution)/shard_map/ppermute | solution.py:17
  287.3 33.8 %collective-permute-start.11 = (f32[32,64]{0,1:T(8,128)S(1)}, f32[32,64]{0,1:T(8,128)S(1)}, u32[]{:S(2)}, u32[]{:S(2)}) collective-permute-start(f32[32,64]{0,1:T(8,128)S(1)} %bitcast.115), channel_id=1, source_target_pairs={{3,0},{7,4},{11,8},{15,12},{19,16},{23,20},{27,24},{31,28}} | collective-permute-start | bytes 24584 | tf_op jit(solution)/shard_map/ppermute | solution.py:17
  321.0 2.2 copy-start.2
  345.4 95.6 %collective-permute-start.12 = (f32[1,64]{0,1:T(8,128)S(1)}, f32[1,64]{0,1:T(8,128)S(1)}, u32[]{:S(2)}, u32[]{:S(2)}) collective-permute-start(f32[1,64]{0,1:T(8,128)S(1)} %slice.108), channel_id=1, source_target_pairs={{0,1},{1,2},{2,3},{4,5},{5,6},{6,7},{8,9},{9,10},{10,11},{12,13},{... | collective-permute-start | bytes 776 | tf_op jit(solution)/shard_map/ppermute | solution.py:17
  346.7 94.3 %collective-permute-start.14 = (f32[32,64]{0,1:T(8,128)S(1)}, f32[32,64]{0,1:T(8,128)S(1)}, u32[]{:S(2)}, u32[]{:S(2)}) collective-permute-start(f32[32,64]{0,1:T(8,128)S(1)} %slice.112), channel_id=1, source_target_pairs={{0,3},{4,7},{8,11},{12,15},{16,19},{20,23},{24,27},{28,31}} | collective-permute-start | bytes 24584 | tf_op jit(solution)/shard_map/ppermute | solution.py:17
  348.0 93.0 %collective-permute-start.15 = (f32[96,64]{0,1:T(8,128)S(1)}, f32[96,64]{0,1:T(8,128)S(1)}, u32[]{:S(2)}, u32[]{:S(2)}) collective-permute-start(f32[96,64]{0,1:T(8,128)S(1)} %bitcast.107), channel_id=1, source_target_pairs={{0,2},{1,3},{4,6},{5,7},{8,10},{9,11},{12,14},{13,15},{16,18},{17,... | collective-permute-start | bytes 73736 | tf_op jit(solution)/shard_map/ppermute | solution.py:17
  441.1 35.3 %collective-permute-start.16 = (f32[96,64]{0,1:T(8,128)S(1)}, f32[96,64]{0,1:T(8,128)S(1)}, u32[]{:S(2)}, u32[]{:S(2)}) collective-permute-start(f32[96,64]{0,1:T(8,128)S(1)} %slice.114), channel_id=1, source_target_pairs={{2,0},{3,1},{6,4},{7,5},{10,8},{11,9},{14,12},{15,13},{18,16},{19,... | collective-permute-start | bytes 73736 | tf_op jit(solution)/shard_map/ppermute | solution.py:17
  443.6 32.9 %collective-permute-start.13 = (f32[1,64]{0,1:T(8,128)S(1)}, f32[1,64]{0,1:T(8,128)S(1)}, u32[]{:S(2)}, u32[]{:S(2)}) collective-permute-start(f32[1,64]{0,1:T(8,128)S(1)} %bitcast.120), channel_id=1, source_target_pairs={{1,0},{2,1},{3,2},{5,4},{6,5},{7,6},{9,8},{10,9},{11,10},{13,12},{... | collective-permute-start | bytes 776 | tf_op jit(solution)/shard_map/ppermute | solution.py:17
  447.5 28.9 %collective-permute-start.17 = (f32[32,64]{0,1:T(8,128)S(1)}, f32[32,64]{0,1:T(8,128)S(1)}, u32[]{:S(2)}, u32[]{:S(2)}) collective-permute-start(f32[32,64]{0,1:T(8,128)S(1)} %bitcast.119), channel_id=1, source_target_pairs={{3,0},{7,4},{11,8},{15,12},{19,16},{23,20},{27,24},{31,28}} | collective-permute-start | bytes 24584 | tf_op jit(solution)/shard_map/ppermute | solution.py:17
where the time goes:
time: 487 us; the launch traced here: 478 us
  blocking collectives  354 us (73%)
  matrix products  73.3 us (15%)
  starting transfers between devices  34.7 us (7%)
  other arithmetic  8.03 us (2%)
  local copies, waits for them, and re-layouts  6.05 us (1%)
    psum x3, blocking collectives, on_device(): grad_dst = lax.psum(raw_dst, ('src', 'tm')) / rank_count  187 us
    psum x3, blocking collectives, on_device(): summed_time = lax.psum(raw_time, ('src', 'dst'))  87.6 us
    psum x3, blocking collectives, on_device(): grad_src = lax.psum(raw_src, ('dst', 'tm')) / rank_count  78.8 us
    ppermute x18, starting transfers between devices, passed_along(): return lax.ppermute(block, axis, route)  34.7 us
    dot_general x3, matrix products, on_device(): raw_src = jnp.einsum('ix,rx->ir', residual, dst_time, precision=highest)  26.3 us
    dot_general x3, matrix products, on_device(): model_cells = jnp.dot(src_now, dst_time, precision=highest)  24.7 us
    dot_general x3, matrix products, on_device(): raw_dst = jnp.einsum('ijk,rik->jr', resid_cube, src_time, precision=highest)  13.4 us
  transfers between devices with their start and end apart: 18, of which 0 were waited for; matrix products, arithmetic and copies ran while one was open for 8% of the time, Pallas kernels for 0%

commit v1 on v0

--- a/solution.py
+++ b/solution.py
@@ -76,7 +76,7 @@
         raw_dst = jnp.einsum("ijk,rik->jr", resid_cube, src_time, precision=highest)
         src_dst = src_now.T[:, :, None] * dst_now.T[:, None, :]
         raw_time = jnp.einsum("ijk,rij->kr", resid_cube, src_dst, precision=highest)
-        grad_src = lax.psum(raw_src, ("dst", "tm")) / rank_count
+        grad_src = jnp.sum(lax.all_gather(raw_src, ("dst", "tm")), axis=0) / rank_count
         grad_dst = lax.psum(raw_dst, ("src", "tm")) / rank_count
         summed_time = lax.psum(raw_time, ("src", "dst"))
         grad_time = (summed_time + smoothing(time_now, position)) / rank_count

time: 487 us -> 473 us (0.971)
  matrix products: 73.3 us -> 64.7 us
  blocking collectives: 354 us -> 348 us
    psum x3 -> x0, blocking collectives: 78.8 us -> none  [on_device(): grad_src = lax.psum(raw_src, ('dst', 'tm')) / rank_count]
    all_gather x0 -> x3, blocking collectives: none -> 74.5 us  [on_device(): lax.all_gather(raw_src, ('dst', 'tm'))]
    psum x3, blocking collectives: 187 us -> 174 us  [on_device(): grad_dst = lax.psum(raw_dst, ('src', 'tm')) / rank_count]
    psum x3, blocking collectives: 87.6 us -> 100 us  [on_device(): summed_time = lax.psum(raw_time, ('src', 'dst'))]
    dot_general x3, matrix products: 26.3 us -> 17.8 us  [on_device(): raw_src = jnp.einsum('ix,rx->ir', residual, dst_time, precision=highest)]
  transfers between devices with their start and end apart: 18 -> 18, of which waited for: 0 -> 0; matrix products, arithmetic and copies ran while one was open for 8% -> 6% of each run, Pallas kernels for 0% -> 0%
where the time goes in v1:
time: 473 us; the launch traced here: 463 us
  blocking collectives  348 us (74%)
  matrix products  64.7 us (14%)
  starting transfers between devices  34.4 us (7%)
  other arithmetic  8.1 us (2%)
  local copies, waits for them, and re-layouts  6.05 us (1%)
    psum x3, blocking collectives, on_device(): grad_dst = lax.psum(raw_dst, ('src', 'tm')) / rank_count  174 us
    psum x3, blocking collectives, on_device(): summed_time = lax.psum(raw_time, ('src', 'dst'))  100 us
    all_gather x3, blocking collectives, on_device(): lax.all_gather(raw_src, ('dst', 'tm'))  74.5 us
    ppermute x18, starting transfers between devices, passed_along(): return lax.ppermute(block, axis, route)  34.4 us
    dot_general x3, matrix products, on_device(): model_cells = jnp.dot(src_now, dst_time, precision=highest)  24.7 us
    dot_general x3, matrix products, on_device(): raw_src = jnp.einsum('ix,rx->ir', residual, dst_time, precision=highest)  17.8 us
    dot_general x3, matrix products, on_device(): raw_dst = jnp.einsum('ijk,rik->jr', resid_cube, src_time, precision=highest)  13.4 us
  transfers between devices with their start and end apart: 18, of which 0 were waited for; matrix products, arithmetic and copies ran while one was open for 6% of the time, Pallas kernels for 0%

profile of v1, /device:TPU:27, one launch (start us, length us, event | category | flops | bytes accessed | tf_op | source)
XLA Modules:
  0.0 463.1 jit_solution(10906123563221120208)
XLA Ops:
  0.7 0.9 slice.72
  1.5 1.3 collective-permute-start
  2.8 0.8 slice.76
  3.7 1.3 collective-permute-start.2
  5.0 1.3 collective-permute-start.3
  6.3 2.1 convert.1
  8.4 1.2 broadcast_multiply_fusion.2
  9.6 8.5 %fusion = f32[64,16384]{1,0:T(8,128)S(1)} fusion(f32[64,64]{1,0:T(8,128)S(1)} %copy-done.4, f32[8,8,128,128]{3,2,1,0:T(8,128)S(1)} %bitcast.89, f32[8,8,128,128]{3,2,1,0:T(8,128)S(1)} %convert.1), kind=kOutput, calls=%fused_computation.3 | convolution fusion | flops 806354944 | bytes 12599296 | tf_op jit(solution)/shard_map/dot_general | solution.py:71
  18.2 6.1 %fusion.7 = f32[64,64]{1,0:T(8,128)S(1)} fusion(f32[64,16384]{1,0:T(8,128)S(1)} %fusion, f32[8,8,128,128]{3,2,1,0:T(8,128)S(1)} %bitcast.90), kind=kOutput, calls=%fused_computation.10 | convolution fusion | flops 805306368 | bytes 8404992 | tf_op jit(solution)/shard_map/ix,rx->ir/dot_general | solution.py:73
  24.3 0.7 copy.9
  25.0 2.9 fusion.31
  28.0 4.5 fusion.28
  32.4 58.2 %psum.42 = f32[128,64]{0,1:T(8,128)S(1)} all-reduce(f32[128,64]{0,1:T(8,128)S(1)} %fusion.28), channel_id=1, replica_groups=mesh['src'=4,'dst'=2,'tm'=4] {'src','tm'}, use_global_device_ids=true, to_apply=%region_1.0 | all-reduce | flops 8192 | bytes 65536 | tf_op jit(solution)/shard_map/psum | solution.py:80
  90.7 24.9 %all-gather = f32[512,64]{1,0:T(8,128)S(1)} all-gather(f32[64,64]{1,0:T(8,128)S(1)} %fusion.7), channel_id=2, replica_groups=mesh['src'=4,'dst'=2,'tm'=4] {'dst','tm'}, dimensions={0}, use_global_device_ids=true | all-gather | bytes 147456 | tf_op jit(solution)/shard_map/all_gather | solution.py:79
  115.8 1.9 collective-permute-start.4
  117.8 4.1 collective-permute-start.1
  121.9 1.3 collective-permute-start.5
  123.2 33.8 %psum.43 = f32[128,64]{0,1:T(8,128)S(1)} all-reduce(f32[128,64]{0,1:T(8,128)S(1)} %fusion.31), channel_id=1, replica_groups=mesh['src'=4,'dst'=2,'tm'=4] {'src','dst'}, use_global_device_ids=true, to_apply=%region_2.0 | all-reduce | flops 8192 | bytes 65536 | tf_op jit(solution)/shard_map/psum | solution.py:81
  157.3 1.2 broadcast_multiply_fusion.1
  159.2 8.1 %convolution_subtract_fusion.1 = f32[64,16384]{1,0:T(8,128)S(1)} fusion(f32[64,64]{1,0:T(8,128)S(1)} %multiply_subtract_fusion.2, f32[8,8,128,128]{3,2,1,0:T(8,128)S(1)} %bitcast.91, f32[8,8,128,128]{3,2,1,0:T(8,128)S(1)} %copy-done.1), kind=kOutput, calls=%fused_computation.1 | convolution fusion | flops 806354944 | bytes 12599296 | tf_op jit(solution)/shard_map/dot_general | solution.py:71
  167.3 5.8 %fusion.4 = f32[64,64]{1,0:T(8,128)S(1)} fusion(f32[64,16384]{1,0:T(8,128)S(1)} %convolution_subtract_fusion.1, f32[8,8,128,128]{3,2,1,0:T(8,128)S(1)} %bitcast.92), kind=kOutput, calls=%fused_computation.7 | convolution fusion | flops 805306368 | bytes 8404992 | tf_op jit(solution)/shard_map/ix,rx->ir/dot_general | solution.py:73
  173.1 0.7 copy.11
  173.9 2.9 fusion.37
  176.8 4.5 fusion.34
  181.3 1.3 collective-permute-start.6
  182.6 1.3 collective-permute-start.8
  183.9 1.3 collective-permute-start.9
  185.2 57.7 %psum.44 = f32[128,64]{0,1:T(8,128)S(1)} all-reduce(f32[128,64]{0,1:T(8,128)S(1)} %fusion.34), channel_id=1, replica_groups=mesh['src'=4,'dst'=2,'tm'=4] {'src','tm'}, use_global_device_ids=true, to_apply=%region_4.5 | all-reduce | flops 8192 | bytes 65536 | tf_op jit(solution)/shard_map/psum | solution.py:80
  242.9 24.7 %all-gather.1 = f32[512,64]{1,0:T(8,128)S(1)} all-gather(f32[64,64]{1,0:T(8,128)S(1)} %fusion.4), channel_id=3, replica_groups=mesh['src'=4,'dst'=2,'tm'=4] {'dst','tm'}, dimensions={0}, use_global_device_ids=true | all-gather | bytes 147456 | tf_op jit(solution)/shard_map/all_gather | solution.py:79
  267.8 1.6 collective-permute-start.10
  269.4 5.0 %collective-permute-start.7 = (f32[1,64]{0,1:T(8,128)S(1)}, f32[1,64]{0,1:T(8,128)S(1)}, u32[]{:S(2)}, u32[]{:S(2)}) collective-permute-start(f32[1,64]{0,1:T(8,128)S(1)} %bitcast.124), channel_id=1, source_target_pairs={{1,0},{2,1},{3,2},{5,4},{6,5},{7,6},{9,8},{10,9},{11,10},{13,12},{... | collective-permute-start | bytes 776 | tf_op jit(solution)/shard_map/ppermute | solution.py:17
  274.4 1.3 collective-permute-start.11
  275.7 33.0 %psum.45 = f32[128,64]{0,1:T(8,128)S(1)} all-reduce(f32[128,64]{0,1:T(8,128)S(1)} %fusion.37), channel_id=1, replica_groups=mesh['src'=4,'dst'=2,'tm'=4] {'src','dst'}, use_global_device_ids=true, to_apply=%region_5.6 | all-reduce | flops 8192 | bytes 65536 | tf_op jit(solution)/shard_map/psum | solution.py:81
  309.0 1.2 broadcast_multiply_fusion
  310.9 8.1 %convolution_subtract_fusion = f32[64,16384]{1,0:T(8,128)S(1)} fusion(f32[8,8,128,128]{3,2,1,0:T(8,128)S(1)} %bitcast.85, f32[8,8,128,128]{3,2,1,0:T(8,128)S(1)} %copy-done.2, f32[64,64]{1,0:T(8,128)S(1)} %multiply_subtract_fusion.2, f32[64,64]{1,0:T(8,128)S(1)} %reduce_sum.28), kind=kOutput, calls=%fused_computation | convolution fusion | flops 806363136 | bytes 12615680 | tf_op jit(solution)/shard_map/dot_general | solution.py:71
  319.0 5.8 %fusion.1 = f32[64,64]{1,0:T(8,128)S(1)} fusion(f32[64,16384]{1,0:T(8,128)S(1)} %convolution_subtract_fusion, f32[8,8,128,128]{3,2,1,0:T(8,128)S(1)} %bitcast.86), kind=kOutput, calls=%fused_computation.4 | convolution fusion | flops 805306368 | bytes 8404992 | tf_op jit(solution)/shard_map/ix,rx->ir/dot_general | solution.py:73
  324.8 0.7 copy.13
  325.5 2.9 fusion.43
  328.5 4.5 fusion.40
  333.0 1.3 collective-permute-start.12
  334.3 1.3 collective-permute-start.14
  335.6 1.3 collective-permute-start.15
  336.9 58.0 %psum.46 = f32[128,64]{0,1:T(8,128)S(1)} all-reduce(f32[128,64]{0,1:T(8,128)S(1)} %fusion.40), channel_id=1, replica_groups=mesh['src'=4,'dst'=2,'tm'=4] {'src','tm'}, use_global_device_ids=true, to_apply=%region_7.8 | all-reduce | flops 8192 | bytes 65536 | tf_op jit(solution)/shard_map/psum | solution.py:80
  395.5 24.9 %all-gather.2 = f32[512,64]{1,0:T(8,128)S(1)} all-gather(f32[64,64]{1,0:T(8,128)S(1)} %fusion.1), channel_id=4, replica_groups=mesh['src'=4,'dst'=2,'tm'=4] {'dst','tm'}, dimensions={0}, use_global_device_ids=true | all-gather | bytes 147456 | tf_op jit(solution)/shard_map/all_gather | solution.py:79
  420.6 1.9 collective-permute-start.16
  423.1 4.4 collective-permute-start.13
  427.5 1.3 collective-permute-start.17
  428.8 33.3 %psum.47 = f32[128,64]{0,1:T(8,128)S(1)} all-reduce(f32[128,64]{0,1:T(8,128)S(1)} %fusion.43), channel_id=1, replica_groups=mesh['src'=4,'dst'=2,'tm'=4] {'src','dst'}, use_global_device_ids=true, to_apply=%region_8.9 | all-reduce | flops 8192 | bytes 65536 | tf_op jit(solution)/shard_map/psum | solution.py:81
  (56 shorter events, 4.7 us)
Async XLA Ops:
  0.6 7.8 %copy-start.3 = (f32[128,64]{0,1:T(8,128)S(1)}, f32[128,64]{0,1:T(8,128)}, u32[]{:S(2)}) copy-start(f32[128,64]{0,1:T(8,128)} %param.7) | copy-start | bytes 98308
  0.6 7.8 %copy-start.5 = (f32[128,64]{0,1:T(8,128)S(1)}, f32[128,64]{0,1:T(8,128)}, u32[]{:S(2)}) copy-start(f32[128,64]{0,1:T(8,128)} %param.6) | copy-start | bytes 98308
  1.5 114.1 %collective-permute-start = (f32[1,64]{0,1:T(8,128)S(1)}, f32[1,64]{0,1:T(8,128)S(1)}, u32[]{:S(2)}, u32[]{:S(2)}) collective-permute-start(f32[1,64]{0,1:T(8,128)S(1)} %slice.72), channel_id=1, source_target_pairs={{0,1},{1,2},{2,3},{4,5},{5,6},{6,7},{8,9},{9,10},{10,11},{12,13},{... | collective-permute-start | bytes 776 | tf_op jit(solution)/shard_map/ppermute | solution.py:17
  3.7 112.0 %collective-permute-start.2 = (f32[32,64]{0,1:T(8,128)S(1)}, f32[32,64]{0,1:T(8,128)S(1)}, u32[]{:S(2)}, u32[]{:S(2)}) collective-permute-start(f32[32,64]{0,1:T(8,128)S(1)} %slice.76), channel_id=1, source_target_pairs={{0,3},{4,7},{8,11},{12,15},{16,19},{20,23},{24,27},{28,31}} | collective-permute-start | bytes 24584 | tf_op jit(solution)/shard_map/ppermute | solution.py:17
  5.0 110.7 %collective-permute-start.3 = (f32[96,64]{0,1:T(8,128)}, f32[96,64]{0,1:T(8,128)S(1)}, u32[]{:S(2)}, u32[]{:S(2)}) collective-permute-start(f32[96,64]{0,1:T(8,128)} %bitcast.104), channel_id=1, source_target_pairs={{0,2},{1,3},{4,6},{5,7},{8,10},{9,11},{12,14},{13,15},{16,18},{17,... | collective-permute-start | bytes 73736 | tf_op jit(solution)/shard_map/ppermute | solution.py:17
  6.3 3.3 copy-start.4
  8.4 9.8 %copy-start = (f32[8,8,128,128]{3,2,1,0:T(8,128)}, f32[8,8,128,128]{3,2,1,0:T(8,128)S(1)}, u32[]{:S(2)}) copy-start(f32[8,8,128,128]{3,2,1,0:T(8,128)S(1)} %convert.1) | copy-start | bytes 12582916
  115.8 41.3 %collective-permute-start.4 = (f32[96,64]{0,1:T(8,128)S(1)}, f32[96,64]{0,1:T(8,128)S(1)}, u32[]{:S(2)}, u32[]{:S(2)}) collective-permute-start(f32[96,64]{0,1:T(8,128)S(1)} %slice.98), channel_id=1, source_target_pairs={{2,0},{3,1},{6,4},{7,5},{10,8},{11,9},{14,12},{15,13},{18,16},{19,... | collective-permute-start | bytes 73736 | tf_op jit(solution)/shard_map/ppermute | solution.py:17
  117.8 39.3 %collective-permute-start.1 = (f32[1,64]{0,1:T(8,128)S(1)}, f32[1,64]{0,1:T(8,128)S(1)}, u32[]{:S(2)}, u32[]{:S(2)}) collective-permute-start(f32[1,64]{0,1:T(8,128)S(1)} %bitcast.122), channel_id=1, source_target_pairs={{1,0},{2,1},{3,2},{5,4},{6,5},{7,6},{9,8},{10,9},{11,10},{13,12},{... | collective-permute-start | bytes 776 | tf_op jit(solution)/shard_map/ppermute | solution.py:17
  121.9 35.2 %collective-permute-start.5 = (f32[32,64]{0,1:T(8,128)S(1)}, f32[32,64]{0,1:T(8,128)S(1)}, u32[]{:S(2)}, u32[]{:S(2)}) collective-permute-start(f32[32,64]{0,1:T(8,128)S(1)} %bitcast.121), channel_id=1, source_target_pairs={{3,0},{7,4},{11,8},{15,12},{19,16},{23,20},{27,24},{31,28}} | collective-permute-start | bytes 24584 | tf_op jit(solution)/shard_map/ppermute | solution.py:17
  157.0 2.2 copy-start.1
  181.3 86.3 %collective-permute-start.6 = (f32[1,64]{0,1:T(8,128)S(1)}, f32[1,64]{0,1:T(8,128)S(1)}, u32[]{:S(2)}, u32[]{:S(2)}) collective-permute-start(f32[1,64]{0,1:T(8,128)S(1)} %slice.100), channel_id=1, source_target_pairs={{0,1},{1,2},{2,3},{4,5},{5,6},{6,7},{8,9},{9,10},{10,11},{12,13},{... | collective-permute-start | bytes 776 | tf_op jit(solution)/shard_map/ppermute | solution.py:17
  182.6 85.0 %collective-permute-start.8 = (f32[32,64]{0,1:T(8,128)S(1)}, f32[32,64]{0,1:T(8,128)S(1)}, u32[]{:S(2)}, u32[]{:S(2)}) collective-permute-start(f32[32,64]{0,1:T(8,128)S(1)} %slice.104), channel_id=1, source_target_pairs={{0,3},{4,7},{8,11},{12,15},{16,19},{20,23},{24,27},{28,31}} | collective-permute-start | bytes 24584 | tf_op jit(solution)/shard_map/ppermute | solution.py:17
  183.9 83.8 %collective-permute-start.9 = (f32[96,64]{0,1:T(8,128)S(1)}, f32[96,64]{0,1:T(8,128)S(1)}, u32[]{:S(2)}, u32[]{:S(2)}) collective-permute-start(f32[96,64]{0,1:T(8,128)S(1)} %bitcast.101), channel_id=1, source_target_pairs={{0,2},{1,3},{4,6},{5,7},{8,10},{9,11},{12,14},{13,15},{16,18},{17,... | collective-permute-start | bytes 73736 | tf_op jit(solution)/shard_map/ppermute | solution.py:17
  267.8 40.9 %collective-permute-start.10 = (f32[96,64]{0,1:T(8,128)S(1)}, f32[96,64]{0,1:T(8,128)S(1)}, u32[]{:S(2)}, u32[]{:S(2)}) collective-permute-start(f32[96,64]{0,1:T(8,128)S(1)} %slice.106), channel_id=1, source_target_pairs={{2,0},{3,1},{6,4},{7,5},{10,8},{11,9},{14,12},{15,13},{18,16},{19,... | collective-permute-start | bytes 73736 | tf_op jit(solution)/shard_map/ppermute | solution.py:17
  269.4 39.3 %collective-permute-start.7 = (f32[1,64]{0,1:T(8,128)S(1)}, f32[1,64]{0,1:T(8,128)S(1)}, u32[]{:S(2)}, u32[]{:S(2)}) collective-permute-start(f32[1,64]{0,1:T(8,128)S(1)} %bitcast.124), channel_id=1, source_target_pairs={{1,0},{2,1},{3,2},{5,4},{6,5},{7,6},{9,8},{10,9},{11,10},{13,12},{... | collective-permute-start | bytes 776 | tf_op jit(solution)/shard_map/ppermute | solution.py:17
  274.4 34.3 %collective-permute-start.11 = (f32[32,64]{0,1:T(8,128)S(1)}, f32[32,64]{0,1:T(8,128)S(1)}, u32[]{:S(2)}, u32[]{:S(2)}) collective-permute-start(f32[32,64]{0,1:T(8,128)S(1)} %bitcast.123), channel_id=1, source_target_pairs={{3,0},{7,4},{11,8},{15,12},{19,16},{23,20},{27,24},{31,28}} | collective-permute-start | bytes 24584 | tf_op jit(solution)/shard_map/ppermute | solution.py:17
  308.7 2.2 copy-start.2
  333.0 87.5 %collective-permute-start.12 = (f32[1,64]{0,1:T(8,128)S(1)}, f32[1,64]{0,1:T(8,128)S(1)}, u32[]{:S(2)}, u32[]{:S(2)}) collective-permute-start(f32[1,64]{0,1:T(8,128)S(1)} %slice.108), channel_id=1, source_target_pairs={{0,1},{1,2},{2,3},{4,5},{5,6},{6,7},{8,9},{9,10},{10,11},{12,13},{... | collective-permute-start | bytes 776 | tf_op jit(solution)/shard_map/ppermute | solution.py:17
  334.3 86.2 %collective-permute-start.14 = (f32[32,64]{0,1:T(8,128)S(1)}, f32[32,64]{0,1:T(8,128)S(1)}, u32[]{:S(2)}, u32[]{:S(2)}) collective-permute-start(f32[32,64]{0,1:T(8,128)S(1)} %slice.112), channel_id=1, source_target_pairs={{0,3},{4,7},{8,11},{12,15},{16,19},{20,23},{24,27},{28,31}} | collective-permute-start | bytes 24584 | tf_op jit(solution)/shard_map/ppermute | solution.py:17
  335.6 84.9 %collective-permute-start.15 = (f32[96,64]{0,1:T(8,128)S(1)}, f32[96,64]{0,1:T(8,128)S(1)}, u32[]{:S(2)}, u32[]{:S(2)}) collective-permute-start(f32[96,64]{0,1:T(8,128)S(1)} %bitcast.110), channel_id=1, source_target_pairs={{0,2},{1,3},{4,6},{5,7},{8,10},{9,11},{12,14},{13,15},{16,18},{17,... | collective-permute-start | bytes 73736 | tf_op jit(solution)/shard_map/ppermute | solution.py:17
  420.6 41.6 %collective-permute-start.16 = (f32[96,64]{0,1:T(8,128)S(1)}, f32[96,64]{0,1:T(8,128)S(1)}, u32[]{:S(2)}, u32[]{:S(2)}) collective-permute-start(f32[96,64]{0,1:T(8,128)S(1)} %slice.114), channel_id=1, source_target_pairs={{2,0},{3,1},{6,4},{7,5},{10,8},{11,9},{14,12},{15,13},{18,16},{19,... | collective-permute-start | bytes 73736 | tf_op jit(solution)/shard_map/ppermute | solution.py:17
  423.1 39.1 %collective-permute-start.13 = (f32[1,64]{0,1:T(8,128)S(1)}, f32[1,64]{0,1:T(8,128)S(1)}, u32[]{:S(2)}, u32[]{:S(2)}) collective-permute-start(f32[1,64]{0,1:T(8,128)S(1)} %bitcast.126), channel_id=1, source_target_pairs={{1,0},{2,1},{3,2},{5,4},{6,5},{7,6},{9,8},{10,9},{11,10},{13,12},{... | collective-permute-start | bytes 776 | tf_op jit(solution)/shard_map/ppermute | solution.py:17
  427.5 34.7 %collective-permute-start.17 = (f32[32,64]{0,1:T(8,128)S(1)}, f32[32,64]{0,1:T(8,128)S(1)}, u32[]{:S(2)}, u32[]{:S(2)}) collective-permute-start(f32[32,64]{0,1:T(8,128)S(1)} %bitcast.125), channel_id=1, source_target_pairs={{3,0},{7,4},{11,8},{15,12},{19,16},{23,20},{27,24},{31,28}} | collective-permute-start | bytes 24584 | tf_op jit(solution)/shard_map/ppermute | solution.py:17
